TPU v7x, 256 devices: a whole 4x4x8 slice. The times are simulated.
256 devices in a mesh: req: 64 (over x, z, core), tensor: 4 (over y).
Axes of the slice: x: 4, y: 4, z: 8, core: 2. Of those that a mesh axis runs over, the one named last changes fastest.
Arguments:
- stream: bfloat16 [65536, 2048], P('req', 'tensor'), may hold values from -64 to 64
- target_row: int32 [65536], P('req'), may hold values from -1 to 65535, as said below
- segment_ids: int32 [65536], P('req'), may hold values from -1 to 63, as said below
- cache_slot: int32 [65536], P('req'), may hold values from -1 to 2047, as said below
- norm_gain: bfloat16 [2048], replicated, may hold values from 0.099609375 to 1.8984375
- norm_bias: bfloat16 [2048], replicated, may hold values from -3 to 3
- projection: bfloat16 [2048, 3, 2048], P(None, None, 'tensor'), may hold values from -1 to 1
- output_weight: bfloat16 [2048, 2048], P('tensor'), may hold values from -0.125 to 0.125
- cache_pool: bfloat16 [131072, 2, 2048], P('req', None, 'tensor'), may hold values from -6 to 6
Outputs:
- mixed: bfloat16 [65536, 2048], P('req', 'tensor')
- new_pool: bfloat16 [131072, 2, 2048], P('req', None, 'tensor')
Inputs may be any that keep to these rules, and one draw needn't show every extreme that they name: `target_row`: every live row of the request layout is named by exactly one stream row and no other row is named. A device names at most 16 rows of any one device; in every draw some device receives exactly 16 rows from every device and its 1024 rows are all live. `segment_ids`: within one device's 1024 rows the numbers start at 0 on the first row, rise by one at each new request and never fall; a request's rows are consecutive and never cross devices; -1 only on the rows after the last request. A device holds at most 64 requests, and in every draw some device holds exactly that many. `cache_slot`: live rows of one device have distinct slots; a request's rows fill its pages in order, each page being 16 consecutive slots beginning at a multiple of 16; -1 exactly on rows where segment_ids is -1.
All inputs are finite; a program needn't handle non-finite values.
Results may differ from a plain program's by a relative error of at most 0.008.
Values may be sent and summed in bfloat16 or wider, within the bound.
No kernel may reach another device: no remote copies, remote signals or barrier semaphores. Data moves between devices by JAX's collectives and lax.ppermute only.
A program may use at most 128 MiB of HBM per device.

v0:
```python
import math
import jax
import jax.numpy as jnp
from jax import lax
from jax.sharding import PartitionSpec as P

HDIM = 256
ROT = 64
norm_epsilon = 1e-05
masked_score = -1e30
rotary_base = 10000.0


def layer_norm(values, norm_gain, norm_bias):
    widened = values.astype(jnp.float32)
    row_mean = jnp.mean(widened, axis=-1, keepdims=True)
    centred = widened - row_mean
    row_var = jnp.mean(centred * centred, axis=-1, keepdims=True)
    scaled = centred * lax.rsqrt(row_var + norm_epsilon)
    return (scaled * norm_gain.astype(jnp.float32) + norm_bias.astype(jnp.float32)).astype(
        jnp.bfloat16
    )


def rotary(heads_in, position):
    half_rot = ROT // 2
    exponent = jnp.arange(half_rot, dtype=jnp.float32) * (2.0 / ROT)
    inverse_freq = 1.0 / rotary_base**exponent
    angles = position.astype(jnp.float32)[:, None] * inverse_freq[None, :]
    cosine = jnp.cos(angles)[:, None, :]
    sine_part = jnp.sin(angles)[:, None, :]
    widened = heads_in.astype(jnp.float32)
    row_count = widened.shape[0]
    head_count = widened.shape[1]
    paired = widened[..., :ROT].reshape(row_count, head_count, half_rot, 2)
    even_part = paired[..., 0]
    odd_part = paired[..., 1]
    turned = jnp.stack(
        [even_part * cosine - odd_part * sine_part, odd_part * cosine + even_part * sine_part],
        axis=-1,
    )
    turned = turned.reshape(row_count, head_count, ROT)
    return jnp.concatenate([turned, widened[..., ROT:]], axis=-1).astype(jnp.bfloat16)


def project(split_rows, norm_gain, norm_bias, projection):
    features_all = lax.all_gather(split_rows, "tensor", axis=1, tiled=True)
    normed = layer_norm(features_all, norm_gain, norm_bias)
    flat_weight = projection.reshape(projection.shape[0], projection.shape[1] * projection.shape[2])
    return jnp.dot(normed, flat_weight, preferred_element_type=jnp.float32).astype(jnp.bfloat16)


def masked_softmax(scores, allowed):
    scores = jnp.where(allowed[None], scores, masked_score)
    top_score = jnp.max(scores, axis=-1, keepdims=True)
    raised = jnp.where(allowed[None], jnp.exp(scores - top_score), 0.0)
    row_total = jnp.sum(raised, axis=-1, keepdims=True)
    row_total = jnp.where(row_total > 0.0, row_total, 1.0)
    return (raised / row_total).astype(jnp.bfloat16)


def source_of(wanted, labels):
    matches = labels[None, :] == wanted[:, None]
    label_ids = jnp.arange(labels.shape[0], dtype=jnp.int32)
    source = jnp.sum(jnp.where(matches, label_ids[None, :], 0), axis=1)
    return (source, jnp.any(matches, axis=1))


def shards(
    stream,
    target_row,
    segment_ids,
    cache_slot,
    norm_gain,
    norm_bias,
    projection,
    output_weight,
    cache_pool,
):
    peer_count = lax.axis_size("req")
    row_count = stream.shape[0]
    cap_rows = row_count // peer_count
    head_width = projection.shape[2]
    local_heads = head_width // HDIM
    score_scale = 1.0 / math.sqrt(HDIM)
    row_ids = jnp.arange(row_count, dtype=jnp.int32)
    sends_row = target_row >= 0
    receiver = jnp.where(sends_row, target_row // row_count, peer_count)
    local_row = jnp.where(sends_row, target_row % row_count, -1)
    onehot = (receiver[:, None] == jnp.arange(peer_count, dtype=jnp.int32)[None, :]).astype(
        jnp.bfloat16
    )
    strictly_lower = (row_ids[None, :] < row_ids[:, None]).astype(jnp.bfloat16)
    before_count = jnp.dot(strictly_lower, onehot, preferred_element_type=jnp.float32)
    slot_rank = jnp.sum(before_count * onehot.astype(jnp.float32), axis=1).astype(jnp.int32)
    send_slot = jnp.where(sends_row, receiver * cap_rows + slot_rank, -1)
    buffer_ids = jnp.arange(peer_count * cap_rows, dtype=jnp.int32)
    send_source, send_filled = source_of(buffer_ids, send_slot)
    send_rows = jnp.where(send_filled, local_row[send_source], -1).reshape(peer_count, cap_rows)

    def pack(values):
        buffer = jnp.where(
            send_filled[:, None], jnp.take(values, send_source, axis=0), jnp.zeros((), values.dtype)
        )
        return buffer.reshape(peer_count, cap_rows, values.shape[1])

    def unpack(buffer, arrived_rows):
        arrived_source, arrived_found = source_of(row_ids, arrived_rows.reshape(-1))
        flat_values = buffer.reshape(peer_count * cap_rows, buffer.shape[2])
        return jnp.where(
            arrived_found[:, None],
            jnp.take(flat_values, arrived_source, axis=0),
            jnp.zeros((), buffer.dtype),
        )

    projected = project(stream, norm_gain, norm_bias, projection)
    got_stream, got_projected, got_rows = (
        lax.all_to_all(pack(stream), "req", split_axis=0, concat_axis=0, tiled=True),
        lax.all_to_all(pack(projected), "req", split_axis=0, concat_axis=0, tiled=True),
        lax.all_to_all(send_rows, "req", split_axis=0, concat_axis=0, tiled=True),
    )
    placed = unpack(got_stream, got_rows)
    projected = unpack(got_projected, got_rows)
    is_live = segment_ids >= 0
    allowed = (segment_ids[:, None] == segment_ids[None, :]) & (
        row_ids[None, :] <= row_ids[:, None]
    )
    position = jnp.sum(allowed.astype(jnp.int32), axis=1) - 1
    projected = projected.reshape(row_count, 3, local_heads, HDIM)
    queries = rotary(projected[:, 0], position)
    keys_rot = rotary(projected[:, 1], position)
    values_all = projected[:, 2]
    scores = (
        jnp.einsum("qhd,khd->hqk", queries, keys_rot, preferred_element_type=jnp.float32)
        * score_scale
    )
    weights = masked_softmax(scores, allowed)
    context = jnp.einsum("hqk,khd->qhd", weights, values_all, preferred_element_type=jnp.float32)
    context = context.astype(jnp.bfloat16)
    head_partial = jnp.dot(
        context.reshape(row_count, head_width), output_weight, preferred_element_type=jnp.float32
    )
    summed = lax.psum_scatter(
        head_partial.astype(jnp.bfloat16), "tensor", scatter_dimension=1, tiled=True
    ).astype(jnp.float32)
    mixed_rows = jnp.where(is_live[:, None], placed.astype(jnp.float32) + summed, 0.0).astype(
        jnp.bfloat16
    )
    key_value = jnp.stack(
        [keys_rot.reshape(row_count, head_width), values_all.reshape(row_count, head_width)], axis=1
    )
    pool_ids = jnp.arange(cache_pool.shape[0], dtype=jnp.int32)
    live_slot = jnp.where(is_live, cache_slot, -1)
    pool_source, pool_found = source_of(pool_ids, live_slot)
    new_pool = jnp.where(
        pool_found[:, None, None], jnp.take(key_value, pool_source, axis=0), cache_pool
    )
    return (mixed_rows, new_pool)


def solution(mesh):
    in_specs = (
        P("req", "tensor"),
        P("req"),
        P("req"),
        P("req"),
        P(),
        P(),
        P(None, None, "tensor"),
        P("tensor", None),
        P("req", None, "tensor"),
    )
    out_specs = (P("req", "tensor"), P("req", None, "tensor"))
    return jax.shard_map(shards, mesh=mesh, in_specs=in_specs, out_specs=out_specs, check_vma=False)
```

profile of v0, /device:TPU:1, one launch (start us, length us, event | category | flops | bytes accessed | tf_op | source)
XLA Modules:
  0.0 347.6 jit_solution(13693267671818737325)
XLA Ops:
  10.4 4.5 %gather_fusion = s32[1024]{0:T(1024)S(1)} fusion(s32[1024]{0:T(1024)S(1)} %get-tuple-element.15, s32[1024]{0:T(1024)S(1)} %broadcast_clamp_fusion.1), kind=kCustom, calls=%fused_computation.4 | custom fusion | bytes 12288 | tf_op jit(solution)/shard_map/gather | solution.py:99
  16.2 13.0 %all-to-all-start = ((s32[64,1,16]{2,1,0:T(1,128)}), s32[64,1,16]{2,1,0:T(1,128)S(1)}, u32[]{:S(2)}, u32[]{:S(2)}) async-start(s32[64,1,16]{2,1,0:T(1,128)} %bitcast.2), calls=%async_computation | async-start | bytes 65536 | tf_op jit(solution)/shard_map/all_to_all | solution.py:120
  29.3 8.8 %copy.52 = bf16[2048,3,512]{0,2,1:T(8,128)(2,1)} copy(bf16[2048,3,512]{2,0,1:T(8,128)(2,1)} %param.19) | data formatting | bytes 12582912 | tf_op args[6]
  38.2 26.3 %all-gather.2.cloned.1.call-done = bf16[1024,2048]{1,0:T(8,128)(2,1)} async-done(((bf16[1024,512]{1,0:T(8,128)(2,1)}), bf16[1024,2048]{1,0:T(8,128)(2,1)}) %all-gather.2.cloned.1.call-update) | async-done | bytes 4194320 | tf_op jit(solution)/shard_map/all_gather | solution.py:47
  64.5 3.0 convert_reduce_fusion
  69.2 11.1 %fusion.23 = bf16[1024,1536]{1,0:T(8,128)(2,1)} fusion(bf16[2048,1536]{0,1:T(8,128)(2,1)} %bitcast.36, bf16[1024,2048]{1,0:T(8,128)(2,1)S(1)} %copy-done.2, f32[2048]{0:T(1024)S(1)} %convert_element_type.87, f32[2048]{0:T(1024)S(1)} %convert_element_type.86, f32[1024]{0:T(1024)S(1)} %add_rsqrt_fusion, f32[1024]{0:T(1024)S(1)} %broadcast_multiply_fusion), kind=kOutput, calls=%fused_computation.44 | convolution fusion | flops 6456606720 | bytes 13656064 | tf_op jit(solution)/shard_map/dot_general | solution.py:50
  80.3 9.6 %gather_fusion.4 = bf16[1024,1536]{1,0:T(8,128)(2,1)} fusion(bf16[1024,1536]{1,0:T(8,128)(2,1)} %fusion.23, s32[1024]{0:T(1024)S(1)} %fusion.39), kind=kCustom, calls=%fused_computation.1.clone | custom fusion | bytes 6295552 | tf_op jit(solution)/shard_map/jit(_take)/gather | solution.py:103
  89.9 3.5 %select_select_fusion.1 = bf16[1024,1536]{1,0:T(8,128)(2,1)} fusion(bf16[1024,1536]{1,0:T(8,128)(2,1)} %gather_fusion.4, pred[1024]{0:T(1024)(128)(4,1)S(1)} %compare_and_fusion.2, pred[1024]{0:T(1024)(128)(4,1)S(1)} %fusion.18), kind=kLoop, calls=%fused_computation.47 | loop fusion | flops 3145728 | bytes 6293504 | tf_op jit(solution)/shard_map/jit(_where)/select_n | solution.py:102
  93.4 11.0 %all-to-all-start.2 = ((bf16[64,16,1536]{2,1,0:T(8,128)(2,1)}), bf16[64,16,1536]{2,1,0:T(8,128)(2,1)}, u32[]{:S(2)}, u32[]{:S(2)}) async-start(bf16[64,16,1536]{2,1,0:T(8,128)(2,1)} %bitcast.35), calls=%async_computation.2 | async-start | bytes 6291456 | tf_op jit(solution)/shard_map/all_to_all | solution.py:119
  105.6 1.6 fusion.20
  109.6 68.2 %all-to-all-done.2 = bf16[64,16,1536]{2,1,0:T(8,128)(2,1)} async-done(((bf16[64,16,1536]{2,1,0:T(8,128)(2,1)}), bf16[64,16,1536]{2,1,0:T(8,128)(2,1)}, u32[]{:S(2)}, u32[]{:S(2)}) %all-to-all-start.2) | async-done | bytes 3145760 | tf_op jit(solution)/shard_map/all_to_all | solution.py:119
  177.8 9.6 %gather_fusion.5 = bf16[1024,1536]{1,0:T(8,128)(2,1)} fusion(bf16[1024,1536]{1,0:T(8,128)(2,1)} %bitcast.7, s32[1024]{0:T(1024)S(1)} %fusion.40), kind=kCustom, calls=%fused_computation.3.clone | custom fusion | bytes 6295552 | tf_op jit(solution)/shard_map/jit(_take)/gather | solution.py:112
  187.3 3.5 %select_select_fusion = bf16[1024,1536]{1,0:T(8,128)(2,1)} fusion(bf16[1024,1536]{1,0:T(8,128)(2,1)} %gather_fusion.5, pred[1024]{0:T(1024)(128)(4,1)S(1)} %compare_and_fusion.1, pred[1024]{0:T(1024)(128)(4,1)S(1)} %fusion.17), kind=kLoop, calls=%fused_computation.46 | loop fusion | flops 3145728 | bytes 6293504 | tf_op jit(solution)/shard_map/jit(_where)/select_n | solution.py:110
  190.8 4.7 %copy.53 = bf16[1024,1536]{0,1:T(8,128)(2,1)} copy(bf16[1024,1536]{1,0:T(8,128)(2,1)} %select_select_fusion) | data formatting | bytes 6291456 | tf_op jit(solution)/shard_map/jit(_where)/select_n | solution.py:110
  195.5 3.6 %fusion.46 = (bf16[1024,1,2,256]{0,3,2,1:T(8,128)(2,1)}, bf16[1024,1,2,256]{0,3,2,1:T(8,128)(2,1)}, bf16[1024,2,256]{0,2,1:T(8,128)(2,1)}) fusion(bf16[1024,3,2,256]{0,3,2,1:T(8,128)(2,1)} %bitcast.33), kind=kLoop, calls=%fused_computation.111 | loop fusion | bytes 6291456 | tf_op jit(solution)/shard_map/slice | solution.py:132
  204.0 2.4 copy.57
  208.8 2.0 copy.58
  213.0 1.5 maximum_convert_fusion
  216.9 8.0 %fusion.47 = (f32[2,1024]{1,0:T(2,128)S(1)}, f32[2,1024,1024]{1,2,0:T(8,128)}) fusion(f32[2,1024,1024]{1,2,0:T(8,128)S(1)} %fusion.29, pred[1024,1024]{0,1:T(8,128)(4,1)} %fusion.20), kind=kOutput, calls=%fused_computation.112 | output fusion | flops 14681087 | bytes 17833984 | tf_op jit(solution)/shard_map/sub | solution.py:56
  224.8 5.0 %fusion.26 = bf16[2,256,1024]{2,1,0:T(8,128)(2,1)S(1)} fusion(f32[2,1024,1024]{1,2,0:T(8,128)} %get-tuple-element.18, f32[2,1024]{1,0:T(2,128)S(1)} %compare_select_fusion.1, bf16[1024,3,2,256]{0,3,2,1:T(8,128)(2,1)} %bitcast.34), kind=kOutput, calls=%fused_computation.51 | convolution fusion | flops 1078460416 | bytes 10493952 | tf_op jit(solution)/shard_map/hqk,khd->qhd/dot_general | solution.py:138
  229.8 4.3 %convolution_convert_fusion = bf16[1024,2048]{1,0:T(8,128)(2,1)} fusion(bf16[1024,512]{0,1:T(8,128)(2,1)S(1)} %bitcast.48, bf16[512,2048]{1,0:T(8,128)(2,1)S(1)} %copy-done), kind=kOutput, calls=%fused_computation.45 | convolution fusion | flops 2149580800 | bytes 7340032 | tf_op jit(solution)/shard_map/dot_general | solution.py:140
  235.4 5.1 %gather_fusion.2 = bf16[1024,512]{1,0:T(8,128)(2,1)} fusion(bf16[1024,512]{1,0:T(8,128)(2,1)S(1)} %copy-done.1, s32[1024]{0:T(1024)S(1)} %fusion.39), kind=kCustom, calls=%fused_computation.clone | custom fusion | bytes 2101248 | tf_op jit(solution)/shard_map/jit(_take)/gather | solution.py:103
  240.4 2.7 select_select_fusion.3
  243.1 6.0 %all-to-all-start.1 = ((bf16[64,16,512]{2,1,0:T(8,128)(2,1)}), bf16[64,16,512]{2,1,0:T(8,128)(2,1)S(1)}, u32[]{:S(2)}, u32[]{:S(2)}) async-start(bf16[64,16,512]{2,1,0:T(8,128)(2,1)} %bitcast.38), calls=%async_computation.1 | async-start | bytes 2097152 | tf_op jit(solution)/shard_map/all_to_all | solution.py:118
  251.2 26.5 %all-to-all-done.1 = bf16[64,16,512]{2,1,0:T(8,128)(2,1)S(1)} async-done(((bf16[64,16,512]{2,1,0:T(8,128)(2,1)}), bf16[64,16,512]{2,1,0:T(8,128)(2,1)S(1)}, u32[]{:S(2)}, u32[]{:S(2)}) %all-to-all-start.1) | async-done | bytes 1048608 | tf_op jit(solution)/shard_map/all_to_all | solution.py:118
  277.7 5.1 %gather_fusion.3 = bf16[1024,512]{1,0:T(8,128)(2,1)} fusion(bf16[1024,512]{1,0:T(8,128)(2,1)S(1)} %bitcast.32, s32[1024]{0:T(1024)S(1)} %fusion.40), kind=kCustom, calls=%fused_computation.2.clone | custom fusion | bytes 2101248 | tf_op jit(solution)/shard_map/jit(_take)/gather | solution.py:112
  284.3 6.0 %copy.63 = bf16[1024,1,512]{2,1,0:T(2,128)(2,1)} copy(bf16[1024,1,512]{0,2,1:T(8,128)(2,1)} %bitcast.39) | data formatting | bytes 2097152 | tf_op jit(solution)/shard_map/stack;reshape;squeeze | solution.py:149
  290.2 3.9 %copy.62 = bf16[1024,1,512]{2,1,0:T(2,128)(2,1)} copy(bf16[1024,1,512]{0,2,1:T(8,128)(2,1)S(1)} %bitcast.37) | data formatting | bytes 2097152 | tf_op jit(solution)/shard_map/convert_element_type | solution.py:43
  294.2 6.7 %pad_maximum_fusion = bf16[1024,2,512]{2,1,0:T(2,128)(2,1)} fusion(bf16[1024,1,512]{2,1,0:T(2,128)(2,1)} %copy.63, bf16[1024,1,512]{2,1,0:T(2,128)(2,1)} %copy.62), kind=kLoop, calls=%fused_computation.49 | loop fusion | flops 4194304 | bytes 4194304 | tf_op jit(solution)/shard_map/stack | solution.py:149
  300.9 22.9 %gather_fusion.1 = bf16[2048,2,512]{2,1,0:T(2,128)(2,1)} fusion(bf16[1024,2,512]{2,1,0:T(2,128)(2,1)} %pad_maximum_fusion, s32[2048]{0:T(1024)S(1)} %broadcast_clamp_fusion), kind=kCustom, calls=%fused_computation.5 | custom fusion | bytes 8396800 | tf_op jit(solution)/shard_map/jit(_take)/gather | solution.py:156
  323.8 14.1 %broadcast_select_fusion = bf16[2048,2,512]{2,1,0:T(2,128)(2,1)} fusion(bf16[2048,2,512]{2,1,0:T(2,128)(2,1)} %param.21, pred[2048]{0:T(1024)(128)(4,1)S(1)} %fusion.7, bf16[2048,2,512]{2,1,0:T(2,128)(2,1)} %gather_fusion.1, pred[2048]{0:T(1024)(128)(4,1)S(1)} %compare_and_fusion), kind=kLoop, calls=%fused_computation.21 | loop fusion | flops 4194304 | bytes 12587008 | tf_op jit(solution)/shard_map/jit(_where)/select_n | solution.py:155
  337.9 2.8 select_convert_fusion
  (76 shorter events, 26.2 us)
Async XLA Ops:
  7.2 222.7 %copy-start = (bf16[512,2048]{1,0:T(8,128)(2,1)S(1)}, bf16[512,2048]{1,0:T(8,128)(2,1)}, u32[]{:S(2)}) copy-start(bf16[512,2048]{1,0:T(8,128)(2,1)} %param.20) | copy-start | bytes 6291460
  7.2 57.3 %all-gather.2.cloned.1.call-start = ((), (), s32[]{:S(2)}) async-start(), calls=%async_computation.4 | async-start | bytes 5242880 | tf_op jit(solution)/shard_map/all_gather | solution.py:47
  16.2 77.1 %all-to-all-start = ((s32[64,1,16]{2,1,0:T(1,128)}), s32[64,1,16]{2,1,0:T(1,128)S(1)}, u32[]{:S(2)}, u32[]{:S(2)}) async-start(s32[64,1,16]{2,1,0:T(1,128)} %bitcast.2), calls=%async_computation | async-start | bytes 65536 | tf_op jit(solution)/shard_map/all_to_all | solution.py:120
  29.2 8.9 %copy-start.8 = (bf16[2048]{0:T(1024)(128)(2,1)S(1)}, bf16[2048]{0:T(1024)(128)(2,1)}, u32[]{:S(2)}) copy-start(bf16[2048]{0:T(1024)(128)(2,1)} %param.18) | copy-start | bytes 12292
  29.3 8.9 %copy-start.9 = (bf16[2048]{0:T(1024)(128)(2,1)S(1)}, bf16[2048]{0:T(1024)(128)(2,1)}, u32[]{:S(2)}) copy-start(bf16[2048]{0:T(1024)(128)(2,1)} %param.17) | copy-start | bytes 12292
  64.5 3.4 copy-start.2
  93.3 11.3 %copy-start.7 = (s32[1024]{0:T(1024)S(1)}, s32[1024]{0:T(1024)}, u32[]{:S(2)}) copy-start(s32[1024]{0:T(1024)} %param.15) | copy-start | bytes 12292
  93.4 84.4 %all-to-all-start.2 = ((bf16[64,16,1536]{2,1,0:T(8,128)(2,1)}), bf16[64,16,1536]{2,1,0:T(8,128)(2,1)}, u32[]{:S(2)}, u32[]{:S(2)}) async-start(bf16[64,16,1536]{2,1,0:T(8,128)(2,1)} %bitcast.35), calls=%async_computation.2 | async-start | bytes 6291456 | tf_op jit(solution)/shard_map/all_to_all | solution.py:119
  104.4 233.6 %reduce-scatter.2.cloned.1.call-start = ((), (), s32[]{:S(2)}) async-start(), calls=%async_computation.5 | async-start | bytes 5242880 | tf_op jit(solution)/shard_map/reduce_scatter | solution.py:143
  200.6 1.6 copy-start.5
  210.8 4.8 %copy-start.6 = (bf16[1024,2,192]{0,2,1:T(8,128)(2,1)S(1)}, bf16[1024,2,192]{0,2,1:T(8,128)(2,1)}, u32[]{:S(2)}) copy-start(bf16[1024,2,192]{0,2,1:T(8,128)(2,1)} %slice.68) | copy-start | bytes 2359300
  214.5 1.1 copy-start.3
  234.1 1.2 copy-start.1
  240.4 8.7 %copy-start.10 = (s32[1024]{0:T(1024)S(1)}, s32[1024]{0:T(1024)}, u32[]{:S(2)}) copy-start(s32[1024]{0:T(1024)} %param.16) | copy-start | bytes 12292
  243.1 34.6 %all-to-all-start.1 = ((bf16[64,16,512]{2,1,0:T(8,128)(2,1)}), bf16[64,16,512]{2,1,0:T(8,128)(2,1)S(1)}, u32[]{:S(2)}, u32[]{:S(2)}) async-start(bf16[64,16,512]{2,1,0:T(8,128)(2,1)} %bitcast.38), calls=%async_computation.1 | async-start | bytes 2097152 | tf_op jit(solution)/shard_map/all_to_all | solution.py:118
  323.8 14.1 %copy-start.4 = (bf16[1024,512]{1,0:T(8,128)(2,1)S(1)}, bf16[1024,512]{1,0:T(8,128)(2,1)}, u32[]{:S(2)}) copy-start(bf16[1024,512]{1,0:T(8,128)(2,1)} %gather_fusion.3) | copy-start | bytes 3145732
Sparse Core Ops, SparseCore 0:
  9.8 54.5 all-gather.1
  234.3 45.1 reduce-scatter.1
where the time goes:
time: 349 us; the launch traced here: 348 us
  waiting for transfers between devices  122 us (35%)
  local copies, waits for them, and re-layouts  99.1 us (28%)
  other arithmetic  59.8 us (17%)
  starting transfers between devices  30.3 us (9%)
  matrix products  22.3 us (6%)
  between operations  14.4 us (4%)
    all_to_all x1, waiting for transfers between devices, shards(): lax.all_to_all(pack(projected), 'req', split_axis=0, concat_axis=0, tiled...  68.2 us
    all_to_all x1, waiting for transfers between devices, shards(): lax.all_to_all(pack(stream), 'req', split_axis=0, concat_axis=0, tiled=True)  26.5 us
    all_gather x1, waiting for transfers between devices, project(): features_all = lax.all_gather(split_rows, 'tensor', axis=1, tiled=True)  26.3 us
    gather x1, local copies, waits for them, and re-layouts, shards(): jnp.take(key_value, pool_source, axis=0)  22.9 us
    gather x2, local copies, waits for them, and re-layouts, pack(): jnp.take(values, send_source, axis=0)  14.6 us
    gather x2, local copies, waits for them, and re-layouts, unpack(): jnp.take(flat_values, arrived_source, axis=0)  14.6 us
    select_n x1, other arithmetic, shards(): jnp.where(pool_found[:, None, None], jnp.take(key_value, pool_source, axi...  14.1 us
    unnamed x24, local copies, waits for them, and re-layouts  13.1 us
  transfers between devices with their start and end apart: 5, of which 3 were waited for; matrix products, arithmetic and copies ran while one was open for 35% of the time, Pallas kernels for 0%

commit v1 on v0

--- a/solution.py
+++ b/solution.py
@@ -3,6 +3,7 @@
 import jax.numpy as jnp
 from jax import lax
 from jax.sharding import PartitionSpec as P
+from jax.lax import axis_index, axis_size, ppermute
 
 HDIM = 256
 ROT = 64
@@ -44,7 +45,30 @@
 
 
 def project(split_rows, norm_gain, norm_bias, projection):
-    features_all = lax.all_gather(split_rows, "tensor", axis=1, tiled=True)
+    n_parts = axis_size("tensor")
+    fields = []
+    no = 0
+    while no < n_parts:
+        fields.append((no, (no + 1) % n_parts))
+        no = no + 1
+    stack_in = []
+    no = 0
+    while no < n_parts:
+        stack_in.append((no, (no - 1) % n_parts))
+        no += 1
+    v1, carry_out = ([split_rows], [split_rows])
+    for _ in range(n_parts // 2):
+        v1.append(ppermute(v1[-1], "tensor", fields))
+    tick = 0
+    while tick < (n_parts - 1) // 2:
+        n_now = ppermute(carry_out[-1], "tensor", stack_in)
+        carry_out.append(n_now)
+        tick += 1
+    features_all = jnp.roll(
+        jnp.concatenate([*v1[::-1], *carry_out[1:]], axis=1),
+        (axis_index("tensor") - n_parts // 2) * split_rows.shape[1],
+        axis=1,
+    )
     normed = layer_norm(features_all, norm_gain, norm_bias)
     flat_weight = projection.reshape(projection.shape[0], projection.shape[1] * projection.shape[2])
     return jnp.dot(normed, flat_weight, preferred_element_type=jnp.float32).astype(jnp.bfloat16)

time: 349 us -> 366 us (1.049); the launches traced: 348 us -> 360 us
  waiting for transfers between devices: 122 us -> 101 us
  starting transfers between devices: 30.3 us -> 48 us
  local copies, waits for them, and re-layouts: 99.1 us -> 108 us
  other arithmetic: 59.8 us -> 64.7 us
    all_gather x1 -> x0, waiting for transfers between devices: 26.3 us -> none  [project(): features_all = lax.all_gather(split_rows, 'tensor', axis=1, tiled=True)]
    ppermute x0 -> x3, waiting for transfers between devices: none -> 18.6 us  [the longest x2 18.6 us: project(): v1.append(ppermute(v1[-1], 'tensor', fields))]
    all_to_all x1, waiting for transfers between devices: 68.2 us -> 56.3 us  [shards(): lax.all_to_all(pack(projected), 'req', split_axis=0, concat_axis=0, tiled...]
    reduce_scatter x1, starting transfers between devices: 0.22 us -> 12 us  [shards(): lax.psum_scatter(head_partial.astype(jnp.bfloat16), 'tensor', scatter_dim...]
    unnamed x24 -> x35, local copies, waits for them, and re-layouts: 13.1 us -> 19.2 us
    sub x1, other arithmetic: 7.96 us -> 13.5 us  [masked_softmax(): raised = jnp.where(allowed[None], jnp.exp(scores - top_score), 0.0)]
    ppermute x0 -> x3, starting transfers between devices: none -> 5.28 us  [the longest x2 3.75 us: project(): v1.append(ppermute(v1[-1], 'tensor', fields))]
  transfers between devices with their start and end apart: 5 -> 7, of which waited for: 3 -> 3; matrix products, arithmetic and copies ran while one was open for 35% -> 35% of each run, Pallas kernels for 0% -> 0%
where the time goes in v1:
time: 366 us; the launch traced here: 360 us
  local copies, waits for them, and re-layouts  108 us (30%)
  waiting for transfers between devices  101 us (28%)
  other arithmetic  64.7 us (18%)
  starting transfers between devices  48 us (13%)
  matrix products  23.7 us (6%)
  between operations  14.7 us (4%)
    all_to_all x1, waiting for transfers between devices, shards(): lax.all_to_all(pack(projected), 'req', split_axis=0, concat_axis=0, tiled...  56.3 us
    all_to_all x1, waiting for transfers between devices, shards(): lax.all_to_all(pack(stream), 'req', split_axis=0, concat_axis=0, tiled=True)  26.5 us
    gather x1, local copies, waits for them, and re-layouts, shards(): jnp.take(key_value, pool_source, axis=0)  22.9 us
    unnamed x35, local copies, waits for them, and re-layouts  19.2 us
    ppermute x2, waiting for transfers between devices, project(): v1.append(ppermute(v1[-1], 'tensor', fields))  18.6 us
    gather x2, local copies, waits for them, and re-layouts, pack(): jnp.take(values, send_source, axis=0)  14.7 us
    gather x2, local copies, waits for them, and re-layouts, unpack(): jnp.take(flat_values, arrived_source, axis=0)  14.6 us
    select_n x1, other arithmetic, shards(): jnp.where(pool_found[:, None, None], jnp.take(key_value, pool_source, axi...  14.1 us
  transfers between devices with their start and end apart: 7, of which 3 were waited for; matrix products, arithmetic and copies ran while one was open for 35% of the time, Pallas kernels for 0%

profile of v1, /device:TPU:1, one launch (start us, length us, event | category | flops | bytes accessed | tf_op | source)
XLA Modules:
  0.0 360.2 jit_solution(2202682108734637085)
XLA Ops:
  7.2 2.2 collective-permute-start
  13.4 18.5 %collective-permute-done = bf16[1024,512]{1,0:T(8,128)(2,1)} collective-permute-done((bf16[1024,512]{1,0:T(8,128)(2,1)}, bf16[1024,512]{1,0:T(8,128)(2,1)}, u32[]{:S(2)}, u32[]{:S(2)}) %collective-permute-start) | collective-permute-done | bytes 1048608 | tf_op jit(solution)/shard_map/ppermute | solution.py:61
  33.5 4.5 %gather_fusion = s32[1024]{0:T(1024)S(1)} fusion(s32[1024]{0:T(1024)S(1)} %get-tuple-element.15, s32[1024]{0:T(1024)S(1)} %broadcast_clamp_fusion.1), kind=kCustom, calls=%fused_computation.4 | custom fusion | bytes 12288 | tf_op jit(solution)/shard_map/gather | solution.py:123
  39.3 14.0 %all-to-all-start = ((s32[64,1,16]{2,1,0:T(1,128)}), s32[64,1,16]{2,1,0:T(1,128)S(1)}, u32[]{:S(2)}, u32[]{:S(2)}) async-start(s32[64,1,16]{2,1,0:T(1,128)} %bitcast.2), calls=%async_computation | async-start | bytes 65536 | tf_op jit(solution)/shard_map/all_to_all | solution.py:144
  53.4 8.8 %copy.52 = bf16[2048,3,512]{0,2,1:T(8,128)(2,1)} copy(bf16[2048,3,512]{2,0,1:T(8,128)(2,1)} %param.19) | data formatting | bytes 12582912 | tf_op args[6]
  72.9 9.2 %fusion.23 = bf16[1024,1536]{1,0:T(8,128)(2,1)} fusion(bf16[2048,1536]{0,1:T(8,128)(2,1)S(1)} %bitcast.38, f32[2048]{0:T(1024)S(1)} %convert_element_type.87, f32[2048]{0:T(1024)S(1)} %convert_element_type.86, f32[1024]{0:T(1024)S(1)} %add_rsqrt_fusion, f32[1024]{0:T(1024)S(1)} %broadcast_multiply_fusion, ...), kind=kOutput, calls=%fused_computation.44 | convolution fusion | flops 6456606720 | bytes 13656068 | tf_op jit(solution)/shard_map/dot_general | solution.py:74
  82.0 9.6 %gather_fusion.4 = bf16[1024,1536]{1,0:T(8,128)(2,1)} fusion(bf16[1024,1536]{1,0:T(8,128)(2,1)} %fusion.23, s32[1024]{0:T(1024)S(1)} %fusion.40), kind=kCustom, calls=%fused_computation.1.clone | custom fusion | bytes 6295552 | tf_op jit(solution)/shard_map/jit(_take)/gather | solution.py:127
  91.6 3.5 select_select_fusion.1
  95.1 10.6 %all-to-all-start.2 = ((bf16[64,16,1536]{2,1,0:T(8,128)(2,1)}), bf16[64,16,1536]{2,1,0:T(8,128)(2,1)}, u32[]{:S(2)}, u32[]{:S(2)}) async-start(bf16[64,16,1536]{2,1,0:T(8,128)(2,1)} %bitcast.35), calls=%async_computation.2 | async-start | bytes 6291456 | tf_op jit(solution)/shard_map/all_to_all | solution.py:143
  105.7 12.0 %reduce-scatter.2.cloned.1.call-start = ((), (), s32[]{:S(2)}) async-start(), calls=%async_computation.4 | async-start | bytes 5242880 | tf_op jit(solution)/shard_map/reduce_scatter | solution.py:167
  122.8 56.3 %all-to-all-done.2 = bf16[64,16,1536]{2,1,0:T(8,128)(2,1)} async-done(((bf16[64,16,1536]{2,1,0:T(8,128)(2,1)}), bf16[64,16,1536]{2,1,0:T(8,128)(2,1)}, u32[]{:S(2)}, u32[]{:S(2)}) %all-to-all-start.2) | async-done | bytes 3145760 | tf_op jit(solution)/shard_map/all_to_all | solution.py:143
  179.2 9.6 %gather_fusion.5 = bf16[1024,1536]{1,0:T(8,128)(2,1)} fusion(bf16[1024,1536]{1,0:T(8,128)(2,1)} %bitcast.7, s32[1024]{0:T(1024)S(1)} %fusion.41), kind=kCustom, calls=%fused_computation.3.clone | custom fusion | bytes 6295552 | tf_op jit(solution)/shard_map/jit(_take)/gather | solution.py:136
  188.7 3.5 select_select_fusion
  192.2 4.6 %copy.53 = bf16[1024,1536]{0,1:T(8,128)(2,1)} copy(bf16[1024,1536]{1,0:T(8,128)(2,1)} %select_select_fusion) | data formatting | bytes 6291456 | tf_op jit(solution)/shard_map/jit(_where)/select_n | solution.py:134
  196.9 3.6 fusion.48
  200.5 2.3 copy.66
  208.4 2.4 copy.57
  220.2 4.5 %fusion.30 = f32[2,1024,1024]{1,2,0:T(8,128)} fusion(bf16[1024,2,256]{2,0,1:T(8,128)(2,1)S(1)} %maximum_convert_fusion, bf16[1024,2,192]{0,2,1:T(8,128)(2,1)S(1)} %copy-done.5, bf16[1024,2,64]{0,2,1:T(8,128)(2,1)S(1)} %copy.55), kind=kOutput, calls=%fused_computation.56 | convolution fusion | flops 1075838976 | bytes 10485760 | tf_op jit(solution)/shard_map/qhd,khd->hqk/dot_general | solution.py:158
  224.7 13.5 %fusion.49 = (f32[2,1024]{1,0:T(2,128)S(1)}, f32[2,1024,1024]{1,2,0:T(8,128)}) fusion(f32[2,1024,1024]{1,2,0:T(8,128)} %fusion.30, pred[1024,1024]{0,1:T(8,128)(4,1)S(1)} %copy-done.6), kind=kOutput, calls=%fused_computation.122 | output fusion | flops 14681087 | bytes 17833984 | tf_op jit(solution)/shard_map/sub | solution.py:80
  238.2 5.0 %fusion.27 = bf16[2,256,1024]{2,1,0:T(8,128)(2,1)S(1)} fusion(f32[2,1024,1024]{1,2,0:T(8,128)} %get-tuple-element.18, f32[2,1024]{1,0:T(2,128)S(1)} %compare_select_fusion.1, bf16[1024,3,2,256]{0,3,2,1:T(8,128)(2,1)} %bitcast.34), kind=kOutput, calls=%fused_computation.52 | convolution fusion | flops 1078460416 | bytes 10493952 | tf_op jit(solution)/shard_map/hqk,khd->qhd/dot_general | solution.py:162
  243.2 4.5 %convolution_convert_fusion = bf16[1024,2048]{1,0:T(8,128)(2,1)} fusion(bf16[1024,512]{0,1:T(8,128)(2,1)S(1)} %bitcast.50, bf16[512,2048]{1,0:T(8,128)(2,1)S(1)} %copy-done), kind=kOutput, calls=%fused_computation.45 | convolution fusion | flops 2149580800 | bytes 7340032 | tf_op jit(solution)/shard_map/dot_general | solution.py:164
  247.7 5.1 %gather_fusion.2 = bf16[1024,512]{1,0:T(8,128)(2,1)} fusion(bf16[1024,512]{1,0:T(8,128)(2,1)S(1)} %copy-done.1, s32[1024]{0:T(1024)S(1)} %fusion.40), kind=kCustom, calls=%fused_computation.clone | custom fusion | bytes 2101248 | tf_op jit(solution)/shard_map/jit(_take)/gather | solution.py:127
  252.8 2.6 select_select_fusion.3
  255.4 6.1 %all-to-all-start.1 = ((bf16[64,16,512]{2,1,0:T(8,128)(2,1)}), bf16[64,16,512]{2,1,0:T(8,128)(2,1)S(1)}, u32[]{:S(2)}, u32[]{:S(2)}) async-start(bf16[64,16,512]{2,1,0:T(8,128)(2,1)} %bitcast.40), calls=%async_computation.1 | async-start | bytes 2097152 | tf_op jit(solution)/shard_map/all_to_all | solution.py:142
  263.6 26.5 %all-to-all-done.1 = bf16[64,16,512]{2,1,0:T(8,128)(2,1)S(1)} async-done(((bf16[64,16,512]{2,1,0:T(8,128)(2,1)}), bf16[64,16,512]{2,1,0:T(8,128)(2,1)S(1)}, u32[]{:S(2)}, u32[]{:S(2)}) %all-to-all-start.1) | async-done | bytes 1048608 | tf_op jit(solution)/shard_map/all_to_all | solution.py:142
  290.1 5.1 %gather_fusion.3 = bf16[1024,512]{1,0:T(8,128)(2,1)} fusion(bf16[1024,512]{1,0:T(8,128)(2,1)S(1)} %bitcast.32, s32[1024]{0:T(1024)S(1)} %fusion.41), kind=kCustom, calls=%fused_computation.2.clone | custom fusion | bytes 2101248 | tf_op jit(solution)/shard_map/jit(_take)/gather | solution.py:136
  296.6 3.9 %copy.62 = bf16[1024,1,512]{2,1,0:T(2,128)(2,1)} copy(bf16[1024,1,512]{0,2,1:T(8,128)(2,1)S(1)} %bitcast.39) | data formatting | bytes 2097152 | tf_op jit(solution)/shard_map/convert_element_type | solution.py:44
  300.6 6.0 %copy.63 = bf16[1024,1,512]{2,1,0:T(2,128)(2,1)} copy(bf16[1024,1,512]{0,2,1:T(8,128)(2,1)} %bitcast.41) | data formatting | bytes 2097152 | tf_op jit(solution)/shard_map/stack;reshape;squeeze | solution.py:173
  306.5 6.7 %pad_maximum_fusion = bf16[1024,2,512]{2,1,0:T(2,128)(2,1)} fusion(bf16[1024,1,512]{2,1,0:T(2,128)(2,1)} %copy.63, bf16[1024,1,512]{2,1,0:T(2,128)(2,1)} %copy.62), kind=kLoop, calls=%fused_computation.50 | loop fusion | flops 4194304 | bytes 4194304 | tf_op jit(solution)/shard_map/stack | solution.py:173
  313.3 22.9 %gather_fusion.1 = bf16[2048,2,512]{2,1,0:T(2,128)(2,1)} fusion(bf16[1024,2,512]{2,1,0:T(2,128)(2,1)} %pad_maximum_fusion, s32[2048]{0:T(1024)S(1)} %broadcast_clamp_fusion), kind=kCustom, calls=%fused_computation.5 | custom fusion | bytes 8396800 | tf_op jit(solution)/shard_map/jit(_take)/gather | solution.py:180
  336.2 14.1 %broadcast_select_fusion = bf16[2048,2,512]{2,1,0:T(2,128)(2,1)} fusion(bf16[2048,2,512]{2,1,0:T(2,128)(2,1)} %param.21, pred[2048]{0:T(1024)(128)(4,1)S(1)} %fusion.7, bf16[2048,2,512]{2,1,0:T(2,128)(2,1)} %gather_fusion.1, pred[2048]{0:T(1024)(128)(4,1)S(1)} %compare_and_fusion), kind=kLoop, calls=%fused_computation.21 | loop fusion | flops 4194304 | bytes 12587008 | tf_op jit(solution)/shard_map/jit(_where)/select_n | solution.py:179
  350.3 2.8 select_convert_fusion
  (92 shorter events, 40.9 us)
Async XLA Ops:
  7.2 236.0 %copy-start = (bf16[512,2048]{1,0:T(8,128)(2,1)S(1)}, bf16[512,2048]{1,0:T(8,128)(2,1)}, u32[]{:S(2)}) copy-start(bf16[512,2048]{1,0:T(8,128)(2,1)} %param.20) | copy-start | bytes 6291460
  7.2 24.8 %collective-permute-start = (bf16[1024,512]{1,0:T(8,128)(2,1)}, bf16[1024,512]{1,0:T(8,128)(2,1)}, u32[]{:S(2)}, u32[]{:S(2)}) collective-permute-start(bf16[1024,512]{1,0:T(8,128)(2,1)} %param.13), channel_id=1, source_target_pairs={{0,1},{1,2},{2,3},{3,0},{4,5},{5,6},{6,7},{7,4},{8,9},{9,10},{10,1... | collective-permute-start | bytes 3145736 | tf_op jit(solution)/shard_map/ppermute | solution.py:61
  9.4 55.8 %collective-permute-start.2 = (bf16[1024,512]{1,0:T(8,128)(2,1)}, bf16[1024,512]{1,0:T(8,128)(2,1)}, u32[]{:S(2)}, u32[]{:S(2)}) collective-permute-start(bf16[1024,512]{1,0:T(8,128)(2,1)} %param.13), channel_id=1, source_target_pairs={{0,3},{1,0},{2,1},{3,2},{4,7},{5,4},{6,5},{7,6},{8,11},{9,8},{10,9... | collective-permute-start | bytes 3145736 | tf_op jit(solution)/shard_map/ppermute | solution.py:64
  32.0 30.3 %collective-permute-start.1 = (bf16[1024,512]{1,0:T(8,128)(2,1)}, bf16[1024,512]{1,0:T(8,128)(2,1)}, u32[]{:S(2)}, u32[]{:S(2)}) collective-permute-start(bf16[1024,512]{1,0:T(8,128)(2,1)} %collective-permute-done), channel_id=1, source_target_pairs={{0,1},{1,2},{2,3},{3,0},{4,5},{5,6},{6,7},{7,4},{8,9},{9,10},{10,1... | collective-permute-start | bytes 3145736 | tf_op jit(solution)/shard_map/ppermute | solution.py:61
  39.3 55.8 %all-to-all-start = ((s32[64,1,16]{2,1,0:T(1,128)}), s32[64,1,16]{2,1,0:T(1,128)S(1)}, u32[]{:S(2)}, u32[]{:S(2)}) async-start(s32[64,1,16]{2,1,0:T(1,128)} %bitcast.2), calls=%async_computation | async-start | bytes 65536 | tf_op jit(solution)/shard_map/all_to_all | solution.py:144
  53.3 8.9 %copy-start.8 = (bf16[2048]{0:T(1024)(128)(2,1)S(1)}, bf16[2048]{0:T(1024)(128)(2,1)}, u32[]{:S(2)}) copy-start(bf16[2048]{0:T(1024)(128)(2,1)} %param.17) | copy-start | bytes 12292
  53.4 8.9 %copy-start.9 = (bf16[2048]{0:T(1024)(128)(2,1)S(1)}, bf16[2048]{0:T(1024)(128)(2,1)}, u32[]{:S(2)}) copy-start(bf16[2048]{0:T(1024)(128)(2,1)} %param.18) | copy-start | bytes 12292
  62.2 2.9 copy-start.1
  69.3 3.5 slice-start
  70.9 1.9 slice-start.1
  95.1 22.7 %copy-start.7 = (s32[1024]{0:T(1024)S(1)}, s32[1024]{0:T(1024)}, u32[]{:S(2)}) copy-start(s32[1024]{0:T(1024)} %param.15) | copy-start | bytes 12292
  95.1 84.1 %all-to-all-start.2 = ((bf16[64,16,1536]{2,1,0:T(8,128)(2,1)}), bf16[64,16,1536]{2,1,0:T(8,128)(2,1)}, u32[]{:S(2)}, u32[]{:S(2)}) async-start(bf16[64,16,1536]{2,1,0:T(8,128)(2,1)} %bitcast.35), calls=%async_computation.2 | async-start | bytes 6291456 | tf_op jit(solution)/shard_map/all_to_all | solution.py:143
  105.7 244.5 %reduce-scatter.2.cloned.1.call-start = ((), (), s32[]{:S(2)}) async-start(), calls=%async_computation.4 | async-start | bytes 5242880 | tf_op jit(solution)/shard_map/reduce_scatter | solution.py:167
  202.7 3.9 %copy-start.4 = (bf16[1024,2,256]{0,2,1:T(8,128)(2,1)S(1)}, bf16[1024,2,256]{0,2,1:T(8,128)(2,1)}, u32[]{:S(2)}) copy-start(bf16[1024,2,256]{0,2,1:T(8,128)(2,1)} %get-tuple-element.8) | copy-start | bytes 3145732
  215.1 5.1 %copy-start.5 = (bf16[1024,2,192]{0,2,1:T(8,128)(2,1)S(1)}, bf16[1024,2,192]{0,2,1:T(8,128)(2,1)}, u32[]{:S(2)}) copy-start(bf16[1024,2,192]{0,2,1:T(8,128)(2,1)} %slice.68) | copy-start | bytes 2359300
  219.2 1.0 copy-start.2
  220.2 4.5 %copy-start.6 = (pred[1024,1024]{0,1:T(8,128)(4,1)S(1)}, pred[1024,1024]{0,1:T(8,128)(4,1)}, u32[]{:S(2)}) copy-start(pred[1024,1024]{0,1:T(8,128)(4,1)} %fusion.20) | copy-start | bytes 3145732
  252.8 8.7 %copy-start.10 = (s32[1024]{0:T(1024)S(1)}, s32[1024]{0:T(1024)}, u32[]{:S(2)}) copy-start(s32[1024]{0:T(1024)} %param.16) | copy-start | bytes 12292
  255.4 34.6 %all-to-all-start.1 = ((bf16[64,16,512]{2,1,0:T(8,128)(2,1)}), bf16[64,16,512]{2,1,0:T(8,128)(2,1)S(1)}, u32[]{:S(2)}, u32[]{:S(2)}) async-start(bf16[64,16,512]{2,1,0:T(8,128)(2,1)} %bitcast.40), calls=%async_computation.1 | async-start | bytes 2097152 | tf_op jit(solution)/shard_map/all_to_all | solution.py:142
  336.2 14.1 %copy-start.3 = (bf16[1024,512]{1,0:T(8,128)(2,1)S(1)}, bf16[1024,512]{1,0:T(8,128)(2,1)}, u32[]{:S(2)}) copy-start(bf16[1024,512]{1,0:T(8,128)(2,1)} %gather_fusion.3) | copy-start | bytes 3145732
Sparse Core Ops, SparseCore 0:
  247.8 46.0 reduce-scatter.1
